TPU v7x, 128 devices: a whole 4x4x4 slice. The times are simulated.
128 devices in a mesh: req: 16 (over x, z), exp: 8 (over y, core).
Axes of the slice: x: 4, y: 4, z: 4, core: 2. Of those that a mesh axis runs over, the one named last changes fastest.
Arguments:
- tokens: bfloat16 [16384, 2048], P('req'), may hold values from -40 to 40
- routes: int32 [16384, 2], P('req'), may hold values from 0 to 7, all different within a row; in each aligned block of 1024 rows (0 to 1023, 1024 to 2047, ...) at most 320 rows name the same one
- lengths: int32 [64], P('req'), may hold values from 1 to 256, 8192 in all
- cached_prefix_length: int32 [64], P('req'), may hold values from 0 to 64, as said below
- prefix_cache_row: int32 [64], replicated, may hold values from 0 to 15, as said below
- adapter_per_request: int32 [64], P('req'), may hold values from 0 to 63
- adapter_storage_slot: int32 [64], replicated, may hold values from 0 to 63, each once
- router_weight: bfloat16 [2048, 8], replicated, may hold values from -0.125 to 0.125
- key_value_weight: bfloat16 [2048, 4096], P('req', 'exp'), may hold values from -0.125 to 0.125
- expert_query_weight: bfloat16 [2048, 8, 2048], P('req', None, 'exp'), may hold values from -0.125 to 0.125
- expert_output_weight: bfloat16 [8, 2048, 2048], P(None, 'exp', 'req'), may hold values from -0.125 to 0.125
- adapter_down_maps: bfloat16 [64, 2048, 16], P('req'), may hold values from -0.125 to 0.125
- adapter_up_maps: bfloat16 [64, 16, 4096], P('req', None, 'exp'), may hold values from -1.5 to 1.5
- prefix_cache_store: bfloat16 [64, 64, 4096], P('req', None, 'exp'), may hold values from -6 to 6
Outputs:
- attention_out: bfloat16 [16384, 2048], P('req', 'exp')
Inputs may be any that keep to these rules, and one draw needn't show every extreme that they name: `routes`: in each aligned block of 1024 rows (one group) no expert is named by more than 320 rows, and one is named by exactly 320. The lengths sum to 8192 and some request has exactly 256. `cached_prefix_length`: exactly 32 requests have no cached prefix; some request has exactly 64. `prefix_cache_row`: request j of a group keeps its cache in slot j of its row; each row holds exactly one cache in each slot, and no row holds two caches of one group. `adapter_storage_slot`: each slot holds one adapter.
All inputs are finite; a program needn't handle non-finite values. No bound on the sum of `lengths` on one device may be relied on, other than what follows from the above.
Results may differ from a plain program's by a relative error of at most 0.017.
The roundings to bfloat16 on the way count: a program that leaves them out, or rounds other values in their place, can miss the bound.
Values may be sent and summed in bfloat16 or wider, within the bound.
No kernel may reach another device: no remote copies, remote signals or barrier semaphores. Data moves between devices by JAX's collectives and lax.ppermute only.
A program may use at most 128 MiB of HBM per device.

v0:
```python
import jax
import jax.numpy as jnp
from jax import lax
from jax.sharding import PartitionSpec as P

HD = 128
NE = 8
TOPK = 2
CAP = 320
adapter_scale = 0.5


def compact(routes):
    route_flat = routes.reshape(-1)
    pair_count = route_flat.shape[0]
    one_hot = (route_flat[:, None] == jnp.arange(NE, dtype=jnp.int32)[None, :]).astype(jnp.int32)
    earlier = jnp.cumsum(one_hot, axis=0) - one_hot
    route_rank = jnp.sum(earlier * one_hot, axis=1)
    slot_table = (
        jnp.zeros((NE, CAP), jnp.int32)
        .at[route_flat, route_rank]
        .set(jnp.arange(pair_count, dtype=jnp.int32))
    )
    return (route_flat, route_rank, slot_table)


def attend(queries, all_keys, cached_prefix_length):
    per_request = queries.shape[1]
    key_span = all_keys.shape[1]
    cached = key_span - per_request
    scores = jnp.einsum(
        "rtjhd,rshd->rhtjs", queries, all_keys[:, :, :, 0, :], preferred_element_type=jnp.float32
    ) * queries.shape[-1] ** (-0.5)
    key_place = jnp.arange(key_span, dtype=jnp.int32)
    query_place = jnp.arange(per_request, dtype=jnp.int32)
    from_cache = key_place[None, :] < cached_prefix_length[:, None]
    from_prompt = (key_place[None, :] >= cached) & (
        key_place[None, :] - cached <= query_place[:, None]
    )
    allowed = jnp.where(
        key_place[None, None, :] < cached, from_cache[:, None, :], from_prompt[None, :, :]
    )
    allowed = allowed[:, None, :, None, :]
    row_max = jnp.max(jnp.where(allowed, scores, -jnp.inf), axis=-1, keepdims=True)
    weights = jnp.where(allowed, jnp.exp(scores - row_max), 0.0)
    probability = (weights / jnp.sum(weights, axis=-1, keepdims=True)).astype(jnp.bfloat16)
    return jnp.einsum(
        "rhtjs,rshd->rtjhd",
        probability,
        all_keys[:, :, :, 1, :],
        preferred_element_type=jnp.float32,
    ).astype(jnp.bfloat16)


def body(
    tokens,
    routes,
    lengths,
    cached_prefix_length,
    prefix_cache_row,
    adapter_per_request,
    adapter_storage_slot,
    router_weight,
    key_value_weight,
    expert_query_weight,
    expert_output_weight,
    adapter_down_maps,
    adapter_up_maps,
    prefix_cache_store,
):
    group_index = lax.axis_index("req")
    num_requests = lengths.shape[0]
    tok_rows = tokens.shape[0]
    per_request = tok_rows // num_requests
    model_width = tokens.shape[1]
    kv_cols = key_value_weight.shape[1]
    query_cols = expert_query_weight.shape[2]
    heads = kv_cols // (2 * HD)
    cached = prefix_cache_store.shape[1]
    route_flat, route_rank, slot_table = compact(routes)
    picked = tokens[slot_table // 2]
    pieces = (
        lax.all_gather(key_value_weight, "req", axis=0, tiled=True),
        lax.all_gather(expert_query_weight, "req", axis=0, tiled=True),
    )
    key_value_segment = jnp.dot(tokens, pieces[0], preferred_element_type=jnp.float32)
    query_run = jnp.einsum("kcd,dkh->kch", picked, pieces[1], preferred_element_type=jnp.float32)
    adapter_hot = (
        adapter_per_request[:, None]
        == jnp.arange(adapter_storage_slot.shape[0], dtype=jnp.int32)[None, :]
    ).astype(jnp.int32)
    wanted = jnp.sum(adapter_hot * adapter_storage_slot[None, :], axis=1)
    pieces = (
        lax.all_gather(adapter_down_maps, "req", axis=0, tiled=True),
        lax.all_gather(adapter_up_maps, "req", axis=0, tiled=True),
    )
    row_count = pieces[0].shape[0]
    matches = (wanted[:, None] == jnp.arange(row_count, dtype=jnp.int32)[None, :]).astype(
        jnp.bfloat16
    )
    down_run = jnp.einsum("rn,ndq->rdq", matches, pieces[0], preferred_element_type=jnp.float32)
    up_run = jnp.einsum("rn,nqc->rqc", matches, pieces[1], preferred_element_type=jnp.float32)
    reduced_rank_state = jnp.einsum(
        "rtd,rdq->rtq",
        tokens.reshape(num_requests, per_request, model_width),
        down_run.astype(jnp.bfloat16),
        preferred_element_type=jnp.float32,
    ).astype(jnp.bfloat16)
    adapter_term = jnp.einsum(
        "mdg,mgy->mdy",
        reduced_rank_state,
        up_run.astype(jnp.bfloat16),
        preferred_element_type=jnp.float32,
    ).reshape(tok_rows, kv_cols)
    fresh_key_value = (key_value_segment + adapter_scale * adapter_term).astype(jnp.bfloat16)
    own_rows = lax.dynamic_slice_in_dim(
        prefix_cache_row, group_index * num_requests, num_requests, 0
    )
    wanted_slot = own_rows * num_requests + jnp.arange(num_requests, dtype=jnp.int32)
    shard_piece = lax.all_gather(prefix_cache_store, "req", axis=0, tiled=True)
    row_count = shard_piece.shape[0]
    matches = (wanted_slot[:, None] == jnp.arange(row_count, dtype=jnp.int32)[None, :]).astype(
        jnp.bfloat16
    )
    stored = jnp.einsum(
        "rn,nsc->rsc", matches, shard_piece, preferred_element_type=jnp.float32
    ).astype(jnp.bfloat16)
    all_keys = jnp.concatenate(
        [stored, fresh_key_value.reshape(num_requests, per_request, kv_cols)], axis=1
    )
    all_keys = all_keys.reshape(num_requests, cached + per_request, heads, 2, HD)
    queries = query_run.astype(jnp.bfloat16)[route_flat, route_rank].reshape(
        num_requests, per_request, TOPK, heads, HD
    )
    attended = attend(queries, all_keys, cached_prefix_length)
    gathered = attended.reshape(TOPK * tok_rows, query_cols)[slot_table]
    logits = jnp.dot(tokens, router_weight, preferred_element_type=jnp.float32)
    route_hot = (routes[:, :, None] == jnp.arange(NE, dtype=jnp.int32)[None, None, :]).astype(
        jnp.float32
    )
    chosen = jnp.sum(route_hot * logits[:, None, :], axis=-1)
    gate_values = jax.nn.sigmoid(chosen - chosen[:, ::-1])
    live_rows = (
        (jnp.arange(per_request, dtype=jnp.int32)[None, :] < lengths[:, None])
        .reshape(tok_rows)
        .astype(jnp.float32)
    )
    shard_piece = lax.all_gather(expert_output_weight, "req", axis=2, tiled=True)
    out_blocks = jnp.einsum(
        "kch,khn->kcn", gathered, shard_piece, preferred_element_type=jnp.float32
    )
    per_pair = out_blocks[route_flat, route_rank].reshape(tok_rows, TOPK, shard_piece.shape[2])
    partial_value = jnp.sum(per_pair * gate_values[:, :, None], axis=1) * live_rows[:, None]
    return lax.psum_scatter(
        partial_value.astype(jnp.bfloat16), "exp", scatter_dimension=1, tiled=True
    )


def solution(mesh):
    return jax.shard_map(
        body,
        mesh=mesh,
        in_specs=(
            P("req", None),
            P("req", None),
            P("req"),
            P("req"),
            P(),
            P("req"),
            P(),
            P(),
            P("req", "exp"),
            P("req", None, "exp"),
            P(None, "exp", "req"),
            P("req", None, None),
            P("req", None, "exp"),
            P("req", None, "exp"),
        ),
        out_specs=P("req", "exp"),
        check_vma=False,
    )
```

profile of v0, /device:TPU:0, one launch (start us, length us, event | category | flops | bytes accessed | tf_op | source)
XLA Modules:
  0.0 522.8 jit_solution(609906091671764247)
XLA Ops:
  16.9 8.1 %scatter_custom_fusion = s32[2560]{0:T(1024)S(1)} fusion(s32[2048]{0:T(1024)S(1)} %broadcast_select_fusion.1, s32[2048]{0:T(1024)S(1)} %iota.56, s32[]{:T(128)} %constant.20.clone.1), kind=kCustom, calls=%fused_computation.75 | custom fusion | bytes 10244
  25.3 22.9 %gather_fusion = bf16[2560,2048]{1,0:T(8,128)(2,1)} fusion(bf16[1024,2048]{1,0:T(8,128)(2,1)} %param.14, s32[3072]{0:T(1024)S(1)} %pad_clamp_fusion.1), kind=kCustom, calls=%fused_computation | custom fusion | bytes 20981760 | tf_op jit(solution)/shard_map/gather | solution.py:81
  48.2 3.4 fusion.60
  54.8 3.0 convolution_convert_fusion.1
  57.9 50.1 %all-gather.7.cloned.1.call-done = bf16[64,64,512]{2,1,0:T(8,128)(2,1)} async-done(((bf16[4,64,512]{2,1,0:T(8,128)(2,1)}), bf16[64,64,512]{2,1,0:T(8,128)(2,1)}) %all-gather.7.cloned.1.call-update) | async-done | bytes 4194320 | tf_op jit(solution)/shard_map/all_gather | solution.py:120
  107.9 6.7 %fusion.21 = bf16[4,64,512]{2,0,1:T(4,128)(2,1)S(1)} fusion(bf16[64,64,512]{2,1,0:T(8,128)(2,1)} %all-gather.7.cloned.1.call-done, s32[4]{0:T(128)S(1)} %iota_add_fusion.1), kind=kOutput, calls=%fused_computation.29 | convolution fusion | flops 16908544 | bytes 4456464 | tf_op jit(solution)/shard_map/rn,nsc->rsc/dot_general | solution.py:125
  114.8 46.6 %all-gather.11.cloned.1.call-done = bf16[64,2048,16]{1,2,0:T(8,128)(2,1)} async-done(((bf16[4,2048,16]{1,2,0:T(8,128)(2,1)}), bf16[64,2048,16]{1,2,0:T(8,128)(2,1)}) %all-gather.11.cloned.1.call-update) | async-done | bytes 4194320 | tf_op jit(solution)/shard_map/all_gather | solution.py:94
  161.4 6.7 %fusion.15 = bf16[4,2048,16]{1,0,2:T(4,128)(2,1)S(1)} fusion(bf16[64,2048,16]{1,2,0:T(8,128)(2,1)} %all-gather.11.cloned.1.call-done, s32[4]{0:T(128)S(1)} %select_reduce_fusion.2), kind=kOutput, calls=%fused_computation.22 | convolution fusion | flops 16908544 | bytes 4456464 | tf_op jit(solution)/shard_map/rn,ndq->rdq/dot_general | solution.py:101
  168.1 4.0 convolution_multiply_fusion
  172.0 36.2 %all-gather.9.cloned.1.call-done = bf16[2048,512]{1,0:T(8,128)(2,1)} async-done(((bf16[128,512]{1,0:T(8,128)(2,1)}), bf16[2048,512]{1,0:T(8,128)(2,1)}) %all-gather.9.cloned.1.call-update) | async-done | bytes 2097168 | tf_op jit(solution)/shard_map/all_gather | solution.py:83
  208.2 6.2 %fusion.18 = bf16[1024,512]{1,0:T(8,128)(2,1)} fusion(f32[4,256,512]{2,1,0:T(8,128)S(1)} %convolution_multiply_fusion, bf16[1024,2048]{1,0:T(8,128)(2,1)} %param.14, bf16[2048,512]{1,0:T(8,128)(2,1)} %all-gather.9.cloned.1.call-done), kind=kOutput, calls=%fused_computation.24 | convolution fusion | flops 2148532224 | bytes 9437184 | tf_op jit(solution)/shard_map/dot_general | solution.py:86
  216.2 64.2 %all-gather.15.cloned.1.call-done = bf16[2048,8,256]{2,0,1:T(8,128)(2,1)} async-done(((bf16[128,8,256]{2,0,1:T(8,128)(2,1)}), bf16[2048,8,256]{2,0,1:T(8,128)(2,1)}) %all-gather.15.cloned.1.call-update) | async-done | bytes 8388624 | tf_op jit(solution)/shard_map/all_gather | solution.py:84
  280.4 9.2 %convolution_convert_fusion = bf16[8,320,256]{2,1,0:T(8,128)(2,1)S(1)} fusion(bf16[8,320,2048]{2,1,0:T(8,128)(2,1)} %bitcast.79, bf16[2048,8,256]{2,0,1:T(8,128)(2,1)} %all-gather.15.cloned.1.call-done), kind=kOutput, calls=%fused_computation.26 | convolution fusion | flops 2685009920 | bytes 20185088 | tf_op jit(solution)/shard_map/kcd,dkh->kch/dot_general | solution.py:87
  289.7 11.1 %gather_fusion.1 = bf16[2048,256]{1,0:T(8,128)(2,1)S(1)} fusion(bf16[8,320,256]{2,1,0:T(8,128)(2,1)S(1)} %convolution_convert_fusion, s32[2048]{0:T(1024)S(1)} %bitcast.76), kind=kCustom, calls=%fused_computation.1 | custom fusion | bytes 2113536 | tf_op jit(solution)/shard_map/gather | solution.py:132
  301.1 6.3 %fusion.54 = (f32[4,2,256,2]{2,3,1,0:T(2,128)S(1)}, f32[4,2,256,2,320]{2,4,3,1,0:T(8,128)}) fusion(pred[4,256,320]{1,2,0:T(8,128)(4,1)S(1)} %broadcast_select_fusion, bf16[4,256,2,2,128]{4,3,2,1,0:T(2,128)(2,1)S(1)} %reshape.178, bf16[4,320,2,2,128]{4,1,2,0,3:T(8,128)(2,1)} %copy-done.2), kind=kOutput, calls=%fused_computation.96 | convolution fusion | flops 678953280 | bytes 9322496 | tf_op jit(solution)/shard_map/sub | solution.py:45
  307.4 3.3 fusion.20
  311.6 7.6 %gather_fusion.2 = bf16[2560,256]{1,0:T(8,128)(2,1)S(1)} fusion(bf16[2048,256]{1,0:T(8,128)(2,1)S(1)} %bitcast.78, s32[3072]{0:T(1024)S(1)} %pad_clamp_fusion), kind=kCustom, calls=%fused_computation.2 | custom fusion | bytes 2631680 | tf_op jit(solution)/shard_map/gather | solution.py:136
  319.2 41.3 %all-gather.17.cloned.1.call-done = bf16[8,256,2048]{2,1,0:T(8,128)(2,1)} async-done(((bf16[8,256,128]{2,1,0:T(8,128)(2,1)}), bf16[8,256,2048]{2,1,0:T(8,128)(2,1)}) %all-gather.17.cloned.1.call-update) | async-done | bytes 8388624 | tf_op jit(solution)/shard_map/all_gather | solution.py:148
  360.5 12.0 %fusion.59 = f32[8,320,2048]{2,1,0:T(8,128)} fusion(bf16[8,320,256]{2,1,0:T(8,128)(2,1)S(1)} %bitcast.80, bf16[8,256,2048]{2,1,0:T(8,128)(2,1)} %all-gather.17.cloned.1.call-done), kind=kOutput, calls=%fused_computation.97 | convolution fusion | flops 2684354560 | bytes 30670848 | tf_op jit(solution)/shard_map/kch,khn->kcn/dot_general | solution.py:149
  372.5 51.1 %gather_fusion.3 = f32[2048,2048]{1,0:T(8,128)} fusion(f32[8,320,2048]{2,1,0:T(8,128)} %fusion.59, s32[2048]{0:T(1024)S(1)} %bitcast.77), kind=kCustom, calls=%fused_computation.3 | custom fusion | bytes 33570816 | tf_op jit(solution)/shard_map/gather | solution.py:152
  423.6 20.0 %reshape.180 = f32[1024,2,2048]{2,1,0:T(2,128)} reshape(f32[2048,2048]{1,0:T(8,128)} %gather_fusion.3) | data formatting | bytes 33554432 | tf_op jit(solution)/shard_map/reshape | solution.py:152
  443.6 29.1 %multiply_reduce_fusion = f32[1024,2048]{1,0:T(8,128)} fusion(f32[1024,2,2048]{2,1,0:T(2,128)} %reshape.180, f32[1024,2]{1,0:T(8,128)S(1)} %copy.61), kind=kLoop, calls=%fused_computation.6 | loop fusion | flops 6291456 | bytes 25174016 | tf_op jit(solution)/shard_map/reduce_sum | solution.py:153
  472.8 5.8 %multiply_convert_fusion = bf16[1024,2048]{1,0:T(8,128)(2,1)} fusion(f32[1024,2048]{1,0:T(8,128)} %multiply_reduce_fusion, f32[1024]{0:T(1024)S(1)} %bitcast.83), kind=kLoop, calls=%fused_computation.7 | loop fusion | flops 4194304 | bytes 12587008 | tf_op jit(solution)/shard_map/convert_element_type | solution.py:155
  478.6 37.3 %reduce-scatter.2.cloned.1.call-done = bf16[1024,256]{1,0:T(8,128)(2,1)} async-done(((bf16[1024,2048]{1,0:T(8,128)(2,1)}), bf16[1024,256]{1,0:T(8,128)(2,1)}) %reduce-scatter.2.cloned.1.call-update) | async-done | bytes 524304 | tf_op jit(solution)/shard_map/reduce_scatter | solution.py:154
  (82 shorter events, 16.7 us)
Async XLA Ops:
  6.5 41.6 %copy-start = (bf16[2048,8]{0,1:T(8,128)(2,1)S(1)}, bf16[2048,8]{0,1:T(8,128)(2,1)}, u32[]{:S(2)}) copy-start(bf16[2048,8]{0,1:T(8,128)(2,1)} %param.21) | copy-start | bytes 98308
  6.5 10.2 %copy-start.7 = (s32[2]{0:T(128)S(1)}, s32[2]{0:T(128)}, u32[]{:S(2)}) copy-start(s32[2]{0:T(128)} %constant.62) | copy-start | bytes 28
  6.5 10.3 %copy-start.6 = (s32[2]{0:T(128)S(1)}, s32[2]{0:T(128)}, u32[]{:S(2)}) copy-start(s32[2]{0:T(128)} %constant.65) | copy-start | bytes 28
  6.5 48.3 %all-gather.13.cloned.1.call-start = ((), (), s32[]{:S(2)}) async-start(), calls=%async_computation.4 | async-start | bytes 1114112 | tf_op jit(solution)/shard_map/all_gather | solution.py:95
  7.3 100.7 %all-gather.7.cloned.1.call-start = ((), (), s32[]{:S(2)}) async-start(), calls=%async_computation.1 | async-start | bytes 4456448 | tf_op jit(solution)/shard_map/all_gather | solution.py:120
  8.0 153.3 %all-gather.11.cloned.1.call-start = ((), (), s32[]{:S(2)}) async-start(), calls=%async_computation.3 | async-start | bytes 4456448 | tf_op jit(solution)/shard_map/all_gather | solution.py:94
  8.7 199.5 %all-gather.9.cloned.1.call-start = ((), (), s32[]{:S(2)}) async-start(), calls=%async_computation.2 | async-start | bytes 2228224 | tf_op jit(solution)/shard_map/all_gather | solution.py:83
  9.3 271.1 %all-gather.15.cloned.1.call-start = ((), (), s32[]{:S(2)}) async-start(), calls=%async_computation.5 | async-start | bytes 8912896 | tf_op jit(solution)/shard_map/all_gather | solution.py:84
  11.3 349.2 %all-gather.17.cloned.1.call-start = ((), (), s32[]{:S(2)}) async-start(), calls=%async_computation.6 | async-start | bytes 8912896 | tf_op jit(solution)/shard_map/all_gather | solution.py:148
  11.9 504.0 %reduce-scatter.2.cloned.1.call-start = ((), (), s32[]{:S(2)}) async-start(), calls=%async_computation.7 | async-start | bytes 4718592 | tf_op jit(solution)/shard_map/reduce_scatter | solution.py:154
  48.1 3.5 copy-start.4
  48.1 4.2 copy-start.5
  48.1 4.3 copy-start.9
  48.2 4.4 copy-start.10
  48.2 4.4 copy-start.11
  48.2 4.6 copy-start.8
  216.2 64.2 %copy-start.2 = (bf16[4,320,2,2,128]{4,1,2,0,3:T(8,128)(2,1)}, bf16[4,320,2,2,128]{4,1,2,0,3:T(8,128)(2,1)S(1)}, u32[]{:S(2)}) copy-start(bf16[4,320,2,2,128]{4,1,2,0,3:T(8,128)(2,1)S(1)} %copy_dynamic-update-slice_fusion) | copy-start | bytes 3932164
  301.1 6.3 %copy-start.3 = (bf16[4,320,2,2,128]{4,1,2,0,3:T(8,128)(2,1)S(1)}, bf16[4,320,2,2,128]{4,1,2,0,3:T(8,128)(2,1)}, u32[]{:S(2)}) copy-start(bf16[4,320,2,2,128]{4,1,2,0,3:T(8,128)(2,1)} %copy-done.2) | copy-start | bytes 3932164
  472.8 43.2 %copy-start.1 = (bf16[2048,8]{0,1:T(8,128)(2,1)S(1)}, bf16[2048,8]{0,1:T(8,128)(2,1)}, u32[]{:S(2)}) copy-start(bf16[2048,8]{0,1:T(8,128)(2,1)} %param.21) | copy-start | bytes 98308
Sparse Core Ops, SparseCore 0:
  9.5 45.2 all-gather.12
  57.0 50.9 all-gather.6
  110.1 51.2 all-gather.10
  163.4 44.8 all-gather.8
  210.3 70.1 all-gather.14
  282.4 78.0 all-gather.16
  478.7 37.1 reduce-scatter.1
where the time goes:
time: 525 us; the launch traced here: 523 us
  waiting for transfers between devices  280 us (53%)
  local copies, waits for them, and re-layouts  129 us (25%)
  matrix products  60.9 us (12%)
  other arithmetic  38.7 us (7%)
  between operations  13.8 us (3%)
    all_gather x1, waiting for transfers between devices, body(): lax.all_gather(expert_query_weight, 'req', axis=0, tiled=True)  64.2 us
    gather x1, local copies, waits for them, and re-layouts, body(): out_blocks[route_flat, route_rank]  51.1 us
    all_gather x1, waiting for transfers between devices, body(): shard_piece = lax.all_gather(prefix_cache_store, 'req', axis=0, tiled=True)  50.1 us
    all_gather x1, waiting for transfers between devices, body(): lax.all_gather(adapter_down_maps, 'req', axis=0, tiled=True)  46.6 us
    all_gather x1, waiting for transfers between devices, body(): lax.all_gather(expert_output_weight, 'req', axis=2, tiled=True)  41.3 us
    reduce_scatter x1, waiting for transfers between devices, body(): lax.psum_scatter(partial_value.astype(jnp.bfloat16), 'exp', scatter_dimen...  37.3 us
    all_gather x1, waiting for transfers between devices, body(): lax.all_gather(key_value_weight, 'req', axis=0, tiled=True)  36.2 us
    reduce_sum x1, other arithmetic, body(): jnp.sum(per_pair * gate_values[:, :, None], axis=1) * live_rows[:, None]  29.1 us
  transfers between devices with their start and end apart: 7, of which 7 were waited for; matrix products, arithmetic and copies ran while one was open for 21% of the time, Pallas kernels for 0%

commit v1 on v0

--- a/solution.py
+++ b/solution.py
@@ -145,7 +145,12 @@
         .reshape(tok_rows)
         .astype(jnp.float32)
     )
-    shard_piece = lax.all_gather(expert_output_weight, "req", axis=2, tiled=True)
+    ring = [expert_output_weight]
+    for hop in range(15):
+        ring.append(lax.ppermute(ring[-1], "req", [(dev, (dev + 1) % 16) for dev in range(16)]))
+    shard_piece = jnp.roll(
+        jnp.concatenate(ring[::-1], axis=2), (lax.axis_index("req") + 1) * ring[0].shape[2], axis=2
+    )
     out_blocks = jnp.einsum(
         "kch,khn->kcn", gathered, shard_piece, preferred_element_type=jnp.float32
     )

time: 525 us -> 582 us (1.11); the launches traced: 523 us -> 572 us
  local copies, waits for them, and re-layouts: 129 us -> 178 us
  waiting for transfers between devices: 280 us -> 272 us
  other arithmetic: 38.7 us -> 45.3 us
    ppermute x0 -> x15, waiting for transfers between devices: none -> 230 us  [body(): lax.ppermute(ring[-1], 'req', [(dev, (dev + 1) % 16) for dev in range(16)])]
    all_gather x1, waiting for transfers between devices: 64.2 us -> 0.02 us  [body(): lax.all_gather(expert_query_weight, 'req', axis=0, tiled=True)]
    all_gather x1, waiting for transfers between devices: 50.1 us -> 0.01 us  [body(): shard_piece = lax.all_gather(prefix_cache_store, 'req', axis=0, tiled=True)]
    unnamed x30 -> x65, local copies, waits for them, and re-layouts: 11.2 us -> 59.6 us
    all_gather x1, waiting for transfers between devices: 46.6 us -> 0.02 us  [body(): lax.all_gather(adapter_down_maps, 'req', axis=0, tiled=True)]
    all_gather x1 -> x0, waiting for transfers between devices: 41.3 us -> none  [body(): lax.all_gather(expert_output_weight, 'req', axis=2, tiled=True)]
    all_gather x1, waiting for transfers between devices: 36.2 us -> 0.02 us  [body(): lax.all_gather(key_value_weight, 'req', axis=0, tiled=True)]
  transfers between devices with their start and end apart: 7 -> 21, of which waited for: 7 -> 15; matrix products, arithmetic and copies ran while one was open for 21% -> 22% of each run, Pallas kernels for 0% -> 0%
where the time goes in v1:
time: 582 us; the launch traced here: 572 us
  waiting for transfers between devices  272 us (47%)
  local copies, waits for them, and re-layouts  178 us (31%)
  matrix products  60.5 us (10%)
  other arithmetic  45.3 us (8%)
  between operations  14 us (2%)
    ppermute x15, waiting for transfers between devices, body(): lax.ppermute(ring[-1], 'req', [(dev, (dev + 1) % 16) for dev in range(16)])  230 us
    unnamed x65, local copies, waits for them, and re-layouts  59.6 us
    gather x1, local copies, waits for them, and re-layouts, body(): out_blocks[route_flat, route_rank]  51.1 us
    reduce_scatter x1, waiting for transfers between devices, body(): lax.psum_scatter(partial_value.astype(jnp.bfloat16), 'exp', scatter_dimen...  39.1 us
    reduce_sum x1, other arithmetic, body(): jnp.sum(per_pair * gate_values[:, :, None], axis=1) * live_rows[:, None]  30.3 us
    gather x1, local copies, waits for them, and re-layouts, body(): picked = tokens[slot_table // 2]  22.9 us
    reshape x1, local copies, waits for them, and re-layouts, body(): out_blocks[route_flat, route_rank]  20 us
    dot_general x1, matrix products, body(): jnp.einsum('kch,khn->kcn', gathered, shard_piece, preferred_element_type=...  12.2 us
  transfers between devices with their start and end apart: 21, of which 15 were waited for; matrix products, arithmetic and copies ran while one was open for 22% of the time, Pallas kernels for 0%

profile of v1, /device:TPU:0, one launch (start us, length us, event | category | flops | bytes accessed | tf_op | source)
XLA Modules:
  0.0 572.5 jit_solution(11988739281538291947)
XLA Ops:
  13.4 16.8 %collective-permute-done = bf16[8,256,128]{2,1,0:T(8,128)(2,1)S(1)} collective-permute-done((bf16[8,256,128]{2,1,0:T(8,128)(2,1)}, bf16[8,256,128]{2,1,0:T(8,128)(2,1)S(1)}, u32[]{:S(2)}, u32[]{:S(2)}) %collective-permute-start) | collective-permute-done | bytes 524320 | tf_op jit(solution)/shard_map/ppermute | solution.py:150
  30.3 16.5 %collective-permute-done.1 = bf16[8,256,128]{2,1,0:T(8,128)(2,1)S(1)} collective-permute-done((bf16[8,256,128]{2,1,0:T(8,128)(2,1)S(1)}, bf16[8,256,128]{2,1,0:T(8,128)(2,1)S(1)}, u32[]{:S(2)}, u32[]{:S(2)}) %collective-permute-start.1) | collective-permute-done | bytes 524320 | tf_op jit(solution)/shard_map/ppermute | solution.py:150
  46.8 19.6 %collective-permute-done.2 = bf16[8,256,128]{2,1,0:T(8,128)(2,1)S(1)} collective-permute-done((bf16[8,256,128]{2,1,0:T(8,128)(2,1)S(1)}, bf16[8,256,128]{2,1,0:T(8,128)(2,1)S(1)}, u32[]{:S(2)}, u32[]{:S(2)}) %collective-permute-start.2) | collective-permute-done | bytes 524320 | tf_op jit(solution)/shard_map/ppermute | solution.py:150
  66.4 13.5 %collective-permute-done.3 = bf16[8,256,128]{2,1,0:T(8,128)(2,1)S(1)} collective-permute-done((bf16[8,256,128]{2,1,0:T(8,128)(2,1)S(1)}, bf16[8,256,128]{2,1,0:T(8,128)(2,1)S(1)}, u32[]{:S(2)}, u32[]{:S(2)}) %collective-permute-start.3) | collective-permute-done | bytes 524320 | tf_op jit(solution)/shard_map/ppermute | solution.py:150
  79.9 16.8 %collective-permute-done.4 = bf16[8,256,128]{2,1,0:T(8,128)(2,1)S(1)} collective-permute-done((bf16[8,256,128]{2,1,0:T(8,128)(2,1)S(1)}, bf16[8,256,128]{2,1,0:T(8,128)(2,1)S(1)}, u32[]{:S(2)}, u32[]{:S(2)}) %collective-permute-start.4) | collective-permute-done | bytes 524320 | tf_op jit(solution)/shard_map/ppermute | solution.py:150
  96.7 13.7 %collective-permute-done.5 = bf16[8,256,128]{2,1,0:T(8,128)(2,1)S(1)} collective-permute-done((bf16[8,256,128]{2,1,0:T(8,128)(2,1)S(1)}, bf16[8,256,128]{2,1,0:T(8,128)(2,1)S(1)}, u32[]{:S(2)}, u32[]{:S(2)}) %collective-permute-start.5) | collective-permute-done | bytes 524320 | tf_op jit(solution)/shard_map/ppermute | solution.py:150
  110.4 27.3 %collective-permute-done.6 = bf16[8,256,128]{2,1,0:T(8,128)(2,1)} collective-permute-done((bf16[8,256,128]{2,1,0:T(8,128)(2,1)S(1)}, bf16[8,256,128]{2,1,0:T(8,128)(2,1)}, u32[]{:S(2)}, u32[]{:S(2)}) %collective-permute-start.6) | collective-permute-done | bytes 524320 | tf_op jit(solution)/shard_map/ppermute | solution.py:150
  138.9 13.0 %collective-permute-done.7 = bf16[8,256,128]{2,1,0:T(8,128)(2,1)} collective-permute-done((bf16[8,256,128]{2,1,0:T(8,128)(2,1)}, bf16[8,256,128]{2,1,0:T(8,128)(2,1)}, u32[]{:S(2)}, u32[]{:S(2)}) %collective-permute-start.7) | collective-permute-done | bytes 524320 | tf_op jit(solution)/shard_map/ppermute | solution.py:150
  155.4 11.3 %collective-permute-done.8 = bf16[8,256,128]{2,1,0:T(8,128)(2,1)} collective-permute-done((bf16[8,256,128]{2,1,0:T(8,128)(2,1)}, bf16[8,256,128]{2,1,0:T(8,128)(2,1)}, u32[]{:S(2)}, u32[]{:S(2)}) %collective-permute-start.8) | collective-permute-done | bytes 524320 | tf_op jit(solution)/shard_map/ppermute | solution.py:150
  168.3 13.4 %collective-permute-done.9 = bf16[8,256,128]{2,1,0:T(8,128)(2,1)S(1)} collective-permute-done((bf16[8,256,128]{2,1,0:T(8,128)(2,1)}, bf16[8,256,128]{2,1,0:T(8,128)(2,1)S(1)}, u32[]{:S(2)}, u32[]{:S(2)}) %collective-permute-start.9) | collective-permute-done | bytes 524320 | tf_op jit(solution)/shard_map/ppermute | solution.py:150
  181.7 8.1 %scatter_custom_fusion = s32[2560]{0:T(1024)S(1)} fusion(s32[2048]{0:T(1024)S(1)} %broadcast_select_fusion.1, s32[2048]{0:T(1024)S(1)} %iota.56, s32[]{:T(128)} %constant.62.clone.1), kind=kCustom, calls=%fused_computation.109 | custom fusion | bytes 10244
  193.3 15.7 %collective-permute-done.10 = bf16[8,256,128]{2,1,0:T(8,128)(2,1)} collective-permute-done((bf16[8,256,128]{2,1,0:T(8,128)(2,1)S(1)}, bf16[8,256,128]{2,1,0:T(8,128)(2,1)}, u32[]{:S(2)}, u32[]{:S(2)}) %collective-permute-start.10) | collective-permute-done | bytes 524320 | tf_op jit(solution)/shard_map/ppermute | solution.py:150
  211.0 13.2 %collective-permute-done.11 = bf16[8,256,128]{2,1,0:T(8,128)(2,1)} collective-permute-done((bf16[8,256,128]{2,1,0:T(8,128)(2,1)}, bf16[8,256,128]{2,1,0:T(8,128)(2,1)}, u32[]{:S(2)}, u32[]{:S(2)}) %collective-permute-start.11) | collective-permute-done | bytes 524320 | tf_op jit(solution)/shard_map/ppermute | solution.py:150
  225.7 14.6 %collective-permute-done.12 = bf16[8,256,128]{2,1,0:T(8,128)(2,1)S(1)} collective-permute-done((bf16[8,256,128]{2,1,0:T(8,128)(2,1)}, bf16[8,256,128]{2,1,0:T(8,128)(2,1)S(1)}, u32[]{:S(2)}, u32[]{:S(2)}) %collective-permute-start.12) | collective-permute-done | bytes 524320 | tf_op jit(solution)/shard_map/ppermute | solution.py:150
  241.2 24.9 %collective-permute-done.13 = bf16[8,256,128]{2,1,0:T(8,128)(2,1)} collective-permute-done((bf16[8,256,128]{2,1,0:T(8,128)(2,1)S(1)}, bf16[8,256,128]{2,1,0:T(8,128)(2,1)}, u32[]{:S(2)}, u32[]{:S(2)}) %collective-permute-start.13) | collective-permute-done | bytes 524320 | tf_op jit(solution)/shard_map/ppermute | solution.py:150
  267.3 22.9 %gather_fusion = bf16[2560,2048]{1,0:T(8,128)(2,1)} fusion(bf16[1024,2048]{1,0:T(8,128)(2,1)} %param.14, s32[3072]{0:T(1024)S(1)} %get-tuple-element.13), kind=kCustom, calls=%fused_computation | custom fusion | bytes 20981760 | tf_op jit(solution)/shard_map/gather | solution.py:81
  368.0 9.3 %convolution_convert_fusion = bf16[8,320,256]{2,1,0:T(8,128)(2,1)S(1)} fusion(bf16[8,320,2048]{2,1,0:T(8,128)(2,1)} %bitcast.78, bf16[2048,8,256]{2,0,1:T(8,128)(2,1)} %all-gather.14.cloned.1.call-done), kind=kOutput, calls=%fused_computation.28 | convolution fusion | flops 2685009920 | bytes 20185088 | tf_op jit(solution)/shard_map/kcd,dkh->kch/dot_general | solution.py:87
  377.3 11.1 %gather_fusion.1 = bf16[2048,256]{1,0:T(8,128)(2,1)S(1)} fusion(bf16[8,320,256]{2,1,0:T(8,128)(2,1)S(1)} %convolution_convert_fusion, s32[2048]{0:T(1024)S(1)} %bitcast.75), kind=kCustom, calls=%fused_computation.1 | custom fusion | bytes 2113536 | tf_op jit(solution)/shard_map/gather | solution.py:132
  399.2 7.6 %gather_fusion.2 = bf16[2560,256]{1,0:T(8,128)(2,1)S(1)} fusion(bf16[2048,256]{1,0:T(8,128)(2,1)S(1)} %bitcast.77, s32[3072]{0:T(1024)S(1)} %get-tuple-element.12), kind=kCustom, calls=%fused_computation.2 | custom fusion | bytes 2631680 | tf_op jit(solution)/shard_map/gather | solution.py:136
  406.8 12.2 %fusion.1 = f32[8,320,2048]{2,1,0:T(8,128)} fusion(bf16[8,320,256]{2,1,0:T(8,128)(2,1)S(1)} %bitcast.79, bf16[8,256,4096]{2,1,0:T(8,128)(2,1)} %constant_dynamic-update-slice_fusion, s32[]{:T(128)S(6)} %select_n.76), kind=kOutput, calls=%fused_computation.8 | convolution fusion | flops 2684354560 | bytes 30670852 | tf_op jit(solution)/shard_map/kch,khn->kcn/dot_general | solution.py:154
  419.0 51.1 %gather_fusion.3 = f32[2048,2048]{1,0:T(8,128)} fusion(f32[8,320,2048]{2,1,0:T(8,128)} %fusion.1, s32[2048]{0:T(1024)S(1)} %bitcast.76), kind=kCustom, calls=%fused_computation.3 | custom fusion | bytes 33570816 | tf_op jit(solution)/shard_map/gather | solution.py:157
  470.1 20.0 %reshape.180 = f32[1024,2,2048]{2,1,0:T(2,128)} reshape(f32[2048,2048]{1,0:T(8,128)} %gather_fusion.3) | data formatting | bytes 33554432 | tf_op jit(solution)/shard_map/reshape | solution.py:157
  490.1 30.3 %multiply_reduce_fusion = f32[1024,2048]{1,0:T(8,128)} fusion(f32[1024,2,2048]{2,1,0:T(2,128)} %reshape.180, f32[1024,2]{1,0:T(8,128)S(1)} %copy.61), kind=kLoop, calls=%fused_computation.6 | loop fusion | flops 6291456 | bytes 25174016 | tf_op jit(solution)/shard_map/reduce_sum | solution.py:158
  526.3 39.1 %reduce-scatter.2.cloned.1.call-done = bf16[1024,256]{1,0:T(8,128)(2,1)} async-done(((bf16[1024,2048]{1,0:T(8,128)(2,1)}), bf16[1024,256]{1,0:T(8,128)(2,1)}) %reduce-scatter.2.cloned.1.call-update) | async-done | bytes 524304 | tf_op jit(solution)/shard_map/reduce_scatter | solution.py:159
  (144 shorter events, 116.5 us)
Async XLA Ops:
  6.5 183.3 %copy-start = (bf16[2048,8]{0,1:T(8,128)(2,1)S(1)}, bf16[2048,8]{0,1:T(8,128)(2,1)}, u32[]{:S(2)}) copy-start(bf16[2048,8]{0,1:T(8,128)(2,1)} %param.21) | copy-start | bytes 98308
  6.5 284.9 %all-gather.12.cloned.1.call-start = ((), (), s32[]{:S(2)}) async-start(), calls=%async_computation.4 | async-start | bytes 1114112 | tf_op jit(solution)/shard_map/all_gather | solution.py:95
  7.3 334.3 %all-gather.6.cloned.1.call-start = ((), (), s32[]{:S(2)}) async-start(), calls=%async_computation.1 | async-start | bytes 4456448 | tf_op jit(solution)/shard_map/all_gather | solution.py:120
  8.0 340.3 %all-gather.10.cloned.1.call-start = ((), (), s32[]{:S(2)}) async-start(), calls=%async_computation.3 | async-start | bytes 4456448 | tf_op jit(solution)/shard_map/all_gather | solution.py:94
  8.7 350.3 %all-gather.8.cloned.1.call-start = ((), (), s32[]{:S(2)}) async-start(), calls=%async_computation.2 | async-start | bytes 2228224 | tf_op jit(solution)/shard_map/all_gather | solution.py:83
  9.3 357.7 %all-gather.14.cloned.1.call-start = ((), (), s32[]{:S(2)}) async-start(), calls=%async_computation.5 | async-start | bytes 8912896 | tf_op jit(solution)/shard_map/all_gather | solution.py:84
  11.3 554.1 %reduce-scatter.2.cloned.1.call-start = ((), (), s32[]{:S(2)}) async-start(), calls=%async_computation.6 | async-start | bytes 4718592 | tf_op jit(solution)/shard_map/reduce_scatter | solution.py:159
  11.4 18.9 %collective-permute-start = (bf16[8,256,128]{2,1,0:T(8,128)(2,1)}, bf16[8,256,128]{2,1,0:T(8,128)(2,1)S(1)}, u32[]{:S(2)}, u32[]{:S(2)}) collective-permute-start(bf16[8,256,128]{2,1,0:T(8,128)(2,1)} %param.24), channel_id=1, source_target_pairs={{0,8},{8,16},{16,24},{24,32},{32,40},{40,48},{48,56},{56,64},{64,7... | collective-permute-start | bytes 1572872 | tf_op jit(solution)/shard_map/ppermute | solution.py:150
  30.3 16.5 %collective-permute-start.1 = (bf16[8,256,128]{2,1,0:T(8,128)(2,1)S(1)}, bf16[8,256,128]{2,1,0:T(8,128)(2,1)S(1)}, u32[]{:S(2)}, u32[]{:S(2)}) collective-permute-start(bf16[8,256,128]{2,1,0:T(8,128)(2,1)S(1)} %collective-permute-done), channel_id=1, source_target_pairs={{0,8},{8,16},{16,24},{24,32},{32,40},{40,48},{48,56},{56,64},{64,7... | collective-permute-start | bytes 1572872 | tf_op jit(solution)/shard_map/ppermute | solution.py:150
  46.8 19.6 %collective-permute-start.2 = (bf16[8,256,128]{2,1,0:T(8,128)(2,1)S(1)}, bf16[8,256,128]{2,1,0:T(8,128)(2,1)S(1)}, u32[]{:S(2)}, u32[]{:S(2)}) collective-permute-start(bf16[8,256,128]{2,1,0:T(8,128)(2,1)S(1)} %collective-permute-done.1), channel_id=1, source_target_pairs={{0,8},{8,16},{16,24},{24,32},{32,40},{40,48},{48,56},{56,64},{64,7... | collective-permute-start | bytes 1572872 | tf_op jit(solution)/shard_map/ppermute | solution.py:150
  66.4 13.5 %collective-permute-start.3 = (bf16[8,256,128]{2,1,0:T(8,128)(2,1)S(1)}, bf16[8,256,128]{2,1,0:T(8,128)(2,1)S(1)}, u32[]{:S(2)}, u32[]{:S(2)}) collective-permute-start(bf16[8,256,128]{2,1,0:T(8,128)(2,1)S(1)} %collective-permute-done.2), channel_id=1, source_target_pairs={{0,8},{8,16},{16,24},{24,32},{32,40},{40,48},{48,56},{56,64},{64,7... | collective-permute-start | bytes 1572872 | tf_op jit(solution)/shard_map/ppermute | solution.py:150
  79.9 16.8 %collective-permute-start.4 = (bf16[8,256,128]{2,1,0:T(8,128)(2,1)S(1)}, bf16[8,256,128]{2,1,0:T(8,128)(2,1)S(1)}, u32[]{:S(2)}, u32[]{:S(2)}) collective-permute-start(bf16[8,256,128]{2,1,0:T(8,128)(2,1)S(1)} %collective-permute-done.3), channel_id=1, source_target_pairs={{0,8},{8,16},{16,24},{24,32},{32,40},{40,48},{48,56},{56,64},{64,7... | collective-permute-start | bytes 1572872 | tf_op jit(solution)/shard_map/ppermute | solution.py:150
  96.7 193.5 %copy-start.3 = (bf16[8,256,128]{2,1,0:T(8,128)(2,1)}, bf16[8,256,128]{2,1,0:T(8,128)(2,1)S(1)}, u32[]{:S(2)}) copy-start(bf16[8,256,128]{2,1,0:T(8,128)(2,1)S(1)} %collective-permute-done.4) | copy-start | bytes 1572868
  96.7 13.7 %collective-permute-start.5 = (bf16[8,256,128]{2,1,0:T(8,128)(2,1)S(1)}, bf16[8,256,128]{2,1,0:T(8,128)(2,1)S(1)}, u32[]{:S(2)}, u32[]{:S(2)}) collective-permute-start(bf16[8,256,128]{2,1,0:T(8,128)(2,1)S(1)} %collective-permute-done.4), channel_id=1, source_target_pairs={{0,8},{8,16},{16,24},{24,32},{32,40},{40,48},{48,56},{56,64},{64,7... | collective-permute-start | bytes 1572872 | tf_op jit(solution)/shard_map/ppermute | solution.py:150
  110.4 27.3 %collective-permute-start.6 = (bf16[8,256,128]{2,1,0:T(8,128)(2,1)S(1)}, bf16[8,256,128]{2,1,0:T(8,128)(2,1)}, u32[]{:S(2)}, u32[]{:S(2)}) collective-permute-start(bf16[8,256,128]{2,1,0:T(8,128)(2,1)S(1)} %collective-permute-done.5), channel_id=1, source_target_pairs={{0,8},{8,16},{16,24},{24,32},{32,40},{40,48},{48,56},{56,64},{64,7... | collective-permute-start | bytes 1572872 | tf_op jit(solution)/shard_map/ppermute | solution.py:150
  137.7 14.2 %collective-permute-start.7 = (bf16[8,256,128]{2,1,0:T(8,128)(2,1)}, bf16[8,256,128]{2,1,0:T(8,128)(2,1)}, u32[]{:S(2)}, u32[]{:S(2)}) collective-permute-start(bf16[8,256,128]{2,1,0:T(8,128)(2,1)} %collective-permute-done.6), channel_id=1, source_target_pairs={{0,8},{8,16},{16,24},{24,32},{32,40},{40,48},{48,56},{56,64},{64,7... | collective-permute-start | bytes 1572872 | tf_op jit(solution)/shard_map/ppermute | solution.py:150
  151.9 14.8 %collective-permute-start.8 = (bf16[8,256,128]{2,1,0:T(8,128)(2,1)}, bf16[8,256,128]{2,1,0:T(8,128)(2,1)}, u32[]{:S(2)}, u32[]{:S(2)}) collective-permute-start(bf16[8,256,128]{2,1,0:T(8,128)(2,1)} %collective-permute-done.7), channel_id=1, source_target_pairs={{0,8},{8,16},{16,24},{24,32},{32,40},{40,48},{48,56},{56,64},{64,7... | collective-permute-start | bytes 1572872 | tf_op jit(solution)/shard_map/ppermute | solution.py:150
  166.7 14.9 %collective-permute-start.9 = (bf16[8,256,128]{2,1,0:T(8,128)(2,1)}, bf16[8,256,128]{2,1,0:T(8,128)(2,1)S(1)}, u32[]{:S(2)}, u32[]{:S(2)}) collective-permute-start(bf16[8,256,128]{2,1,0:T(8,128)(2,1)} %collective-permute-done.8), channel_id=1, source_target_pairs={{0,8},{8,16},{16,24},{24,32},{32,40},{40,48},{48,56},{56,64},{64,7... | collective-permute-start | bytes 1572872 | tf_op jit(solution)/shard_map/ppermute | solution.py:150
  181.7 27.3 %collective-permute-start.10 = (bf16[8,256,128]{2,1,0:T(8,128)(2,1)S(1)}, bf16[8,256,128]{2,1,0:T(8,128)(2,1)}, u32[]{:S(2)}, u32[]{:S(2)}) collective-permute-start(bf16[8,256,128]{2,1,0:T(8,128)(2,1)S(1)} %collective-permute-done.9), channel_id=1, source_target_pairs={{0,8},{8,16},{16,24},{24,32},{32,40},{40,48},{48,56},{56,64},{64,7... | collective-permute-start | bytes 1572872 | tf_op jit(solution)/shard_map/ppermute | solution.py:150
  209.0 15.2 %collective-permute-start.11 = (bf16[8,256,128]{2,1,0:T(8,128)(2,1)}, bf16[8,256,128]{2,1,0:T(8,128)(2,1)}, u32[]{:S(2)}, u32[]{:S(2)}) collective-permute-start(bf16[8,256,128]{2,1,0:T(8,128)(2,1)} %collective-permute-done.10), channel_id=1, source_target_pairs={{0,8},{8,16},{16,24},{24,32},{32,40},{40,48},{48,56},{56,64},{64,7... | collective-permute-start | bytes 1572872 | tf_op jit(solution)/shard_map/ppermute | solution.py:150
  224.2 16.0 %collective-permute-start.12 = (bf16[8,256,128]{2,1,0:T(8,128)(2,1)}, bf16[8,256,128]{2,1,0:T(8,128)(2,1)S(1)}, u32[]{:S(2)}, u32[]{:S(2)}) collective-permute-start(bf16[8,256,128]{2,1,0:T(8,128)(2,1)} %collective-permute-done.11), channel_id=1, source_target_pairs={{0,8},{8,16},{16,24},{24,32},{32,40},{40,48},{48,56},{56,64},{64,7... | collective-permute-start | bytes 1572872 | tf_op jit(solution)/shard_map/ppermute | solution.py:150
  241.0 25.1 %collective-permute-start.13 = (bf16[8,256,128]{2,1,0:T(8,128)(2,1)S(1)}, bf16[8,256,128]{2,1,0:T(8,128)(2,1)}, u32[]{:S(2)}, u32[]{:S(2)}) collective-permute-start(bf16[8,256,128]{2,1,0:T(8,128)(2,1)S(1)} %collective-permute-done.12), channel_id=1, source_target_pairs={{0,8},{8,16},{16,24},{24,32},{32,40},{40,48},{48,56},{56,64},{64,7... | collective-permute-start | bytes 1572872 | tf_op jit(solution)/shard_map/ppermute | solution.py:150
  266.1 27.9 %collective-permute-start.14 = (bf16[8,256,128]{2,1,0:T(8,128)(2,1)}, bf16[8,256,128]{2,1,0:T(8,128)(2,1)}, u32[]{:S(2)}, u32[]{:S(2)}) collective-permute-start(bf16[8,256,128]{2,1,0:T(8,128)(2,1)} %collective-permute-done.13), channel_id=1, source_target_pairs={{0,8},{8,16},{16,24},{24,32},{32,40},{40,48},{48,56},{56,64},{64,7... | collective-permute-start | bytes 1572872 | tf_op jit(solution)/shard_map/ppermute | solution.py:150
  470.1 95.3 %copy-start.1 = (bf16[2048,8]{0,1:T(8,128)(2,1)S(1)}, bf16[2048,8]{0,1:T(8,128)(2,1)}, u32[]{:S(2)}) copy-start(bf16[2048,8]{0,1:T(8,128)(2,1)} %param.21) | copy-start | bytes 98308
  (11 other events, 328.3 us)
Sparse Core Ops, SparseCore 0:
  9.5 57.5 all-gather.11
  69.3 69.1 all-gather.5
  140.7 71.2 all-gather.9
  213.9 46.2 all-gather.7
  262.3 74.5 all-gather.13
  526.4 38.9 reduce-scatter.1
